TPU v7x, 128 devices: a whole 4x4x4 slice. The times are simulated.
128 devices in a mesh: req: 16 (over z, y), mp: 8 (over x, core).
Axes of the slice: x: 4, y: 4, z: 4, core: 2. Of those that a mesh axis runs over, the one named last changes fastest.
Arguments:
- q_pre: bfloat16 [8192, 3072], P('req', 'mp'), may hold values from -64 to 64
- k_pre: bfloat16 [8192, 1024], P('req', 'mp'), may hold values from -64 to 64
- v_pre: bfloat16 [8192, 1024], P('req', 'mp'), may hold values from -12 to 12
- q_bias: float32 [3072], P('mp'), may hold values from -3 to 3
- k_bias: float32 [1024], P('mp'), may hold values from -3 to 3
- v_bias: float32 [1024], P('mp'), may hold values from -3 to 3
- segment_ids: int32 [8192], P('req'), may hold values from -1 to 63, as said below
- lengths: int32 [16, 4], replicated, may hold values from 64 to 128, as said below
- page_table: int32 [16, 4], replicated, may hold values from 0 to 63, as said below
- w_out: bfloat16 [3072, 5120], P('mp'), may hold values from -0.109375 to 0.109375
- residual: bfloat16 [8192, 5120], P('req'), may hold values from -4 to 4
- norm_gain: float32 [5120], replicated, may hold values from 0.1 to 1.9
- w_gate: bfloat16 [5120, 6912], P('req', 'mp'), may hold values from -0.078125 to 0.078125
- w_up: bfloat16 [5120, 6912], P('req', 'mp'), may hold values from -0.078125 to 0.078125
Outputs:
- hidden: bfloat16 [8192, 6912], P('req', 'mp')
- kv_cache: bfloat16 [64, 8, 128, 256], P('req', 'mp')
Inputs may be any that keep to these rules, and one draw needn't show every extreme that they name: Requests of block r lie in order from the block's first token, request j taking lengths[r, j] tokens; in every block one request has exactly 128 tokens. `segment_ids`: token t of block r carries r * 4 + j inside request j's run of tokens given by lengths, and -1 after the last request of its block. `page_table`: every page is named once; page p is held by req index p // 4; the requests of one block have pages held by different req indices.
All inputs are finite; a program needn't handle non-finite values.
Results may differ from a plain program's by a relative error of at most 0.019.
Values may be sent and summed in bfloat16 or wider, within the bound.
A program may use at most 128 MiB of HBM per device.

v0:
```python
import math
import jax
import jax.numpy as jnp
from jax import lax
from jax.sharding import PartitionSpec as P

HD = 128
PAGE = 128
REQS = 4
THETA = 1000000.0
EPS = 1e-06


def rotate(values, positions):
    half_dim = values.shape[-1] // 2
    frequencies = THETA ** (-jnp.arange(half_dim, dtype=jnp.float32) * (2.0 / values.shape[-1]))
    angles = positions[:, None] * frequencies[None, :]
    cosine = jnp.cos(angles)[:, None, :]
    sine_part = jnp.sin(angles)[:, None, :]
    first_half = values[..., :half_dim]
    second = values[..., half_dim:]
    return jnp.concatenate(
        [first_half * cosine - second * sine_part, second * cosine + first_half * sine_part],
        axis=-1,
    )


def normalize(resid_rows, summed, gain_row):
    state = resid_rows.astype(jnp.float32) + summed
    scale_row = lax.rsqrt(jnp.mean(state * state, axis=-1, keepdims=True) + EPS)
    return (state * scale_row * gain_row).astype(jnp.bfloat16)


def shards(
    q_pre,
    k_pre,
    v_pre,
    q_bias,
    k_bias,
    v_bias,
    segment_ids,
    lengths,
    page_table,
    w_out,
    residual,
    norm_gain,
    w_gate,
    w_up,
):
    me_req = lax.axis_index("req")
    groups_all = lax.axis_size("req")
    block_rows = q_pre.shape[0]
    kv_heads = k_pre.shape[1] // HD
    q_heads = q_pre.shape[1] // HD
    group_size = q_heads // kv_heads
    wg_full = lax.all_gather(w_gate, "req", axis=0, tiled=True)
    wu_full = lax.all_gather(w_up, "req", axis=0, tiled=True)
    own_lens = lax.dynamic_index_in_dim(lengths, me_req, 0, keepdims=False)
    own_pages = lax.dynamic_index_in_dim(page_table, me_req, 0, keepdims=False)
    own_owner = own_pages // REQS
    starts = jnp.cumsum(own_lens) - own_lens
    alive = segment_ids >= 0
    req_idx = jnp.clip(segment_ids - me_req * REQS, 0, REQS - 1)
    req_hit = req_idx[:, None] == jnp.arange(REQS)[None, :]
    row_start = jnp.sum(jnp.where(req_hit, starts[None, :], 0), axis=1)
    token = jnp.arange(block_rows, dtype=jnp.int32)
    positions = (token - row_start).astype(jnp.float32)
    keep = alive[:, None, None]
    queries = rotate(
        (q_pre.astype(jnp.float32) + q_bias).reshape(block_rows, q_heads, HD), positions
    )
    queries = jnp.where(keep, queries, 0.0).astype(jnp.bfloat16)
    keys = rotate((k_pre.astype(jnp.float32) + k_bias).reshape(block_rows, kv_heads, HD), positions)
    keys = jnp.where(keep, keys, 0.0).astype(jnp.bfloat16)
    values = (v_pre.astype(jnp.float32) + v_bias).reshape(block_rows, kv_heads, HD)
    values = jnp.where(keep, values, 0.0).astype(jnp.bfloat16)
    scale_factor = 1.0 / math.sqrt(HD)
    q_groups = queries.reshape(block_rows, kv_heads, group_size, HD)
    scores = (
        jnp.einsum("qhge,khe->hgqk", q_groups, keys, preferred_element_type=jnp.float32)
        * scale_factor
    )
    allowed = (
        (segment_ids[:, None] == segment_ids[None, :])
        & alive[None, :]
        & (token[None, :] <= token[:, None])
    )[None, None]
    row_max = jnp.max(jnp.where(allowed, scores, -1e30), axis=-1, keepdims=True)
    weights = jnp.where(allowed, jnp.exp(scores - row_max), 0.0)
    row_sum = jnp.sum(weights, axis=-1, keepdims=True)
    present = alive[None, None, :, None]
    probs = jnp.where(present, weights / jnp.where(present, row_sum, 1.0), 0.0).astype(jnp.bfloat16)
    attended = jnp.einsum("hgqk,khe->qhge", probs, values, preferred_element_type=jnp.float32)
    attended = attended.astype(jnp.bfloat16).reshape(block_rows, q_heads * HD)
    kv_rows = jnp.concatenate([keys, values], axis=-1)
    kv_rows = jnp.pad(kv_rows, ((0, PAGE), (0, 0), (0, 0)))
    slot = jnp.arange(PAGE, dtype=jnp.int32)
    pages = []
    for j in range(REQS):
        page = lax.dynamic_slice_in_dim(kv_rows, starts[j], PAGE, axis=0)
        page = jnp.where((slot < own_lens[j])[:, None, None], page, jnp.zeros((), jnp.bfloat16))
        pages.append(page)
    pages = jnp.stack(pages)
    to_owner = (own_owner[None, :] == jnp.arange(groups_all)[:, None]).astype(jnp.bfloat16)
    kv_send = jnp.einsum(
        "gj,jphc->gphc", to_owner, pages, preferred_element_type=jnp.float32
    ).astype(jnp.bfloat16)
    kv_in = lax.all_to_all(kv_send, "req", split_axis=0, concat_axis=0, tiled=True)
    hits = (
        page_table[None, :, :] == (me_req * REQS + jnp.arange(REQS, dtype=jnp.int32))[:, None, None]
    )
    page_select = jnp.sum(hits.astype(jnp.int32), axis=2).astype(jnp.bfloat16)
    cache_out = jnp.einsum(
        "ls,sphc->lhpc", page_select, kv_in, preferred_element_type=jnp.float32
    ).astype(jnp.bfloat16)
    summed = lax.psum(
        jnp.dot(attended, w_out, preferred_element_type=jnp.float32).astype(jnp.bfloat16), "mp"
    ).astype(jnp.float32)
    normed = normalize(residual, summed, norm_gain)
    gate_acc = jnp.dot(normed, wg_full, preferred_element_type=jnp.float32)
    up_acc = jnp.dot(normed, wu_full, preferred_element_type=jnp.float32)
    hidden = (jax.nn.silu(gate_acc) * up_acc).astype(jnp.bfloat16)
    return (hidden, cache_out)


def solution(mesh):
    in_specs = (
        P("req", "mp"),
        P("req", "mp"),
        P("req", "mp"),
        P("mp"),
        P("mp"),
        P("mp"),
        P("req"),
        P(),
        P(),
        P("mp", None),
        P("req", None),
        P(),
        P("req", "mp"),
        P("req", "mp"),
    )
    out_specs = (P("req", "mp"), P("req", "mp", None, None))
    return jax.shard_map(shards, mesh=mesh, in_specs=in_specs, out_specs=out_specs, check_vma=False)
```

profile of v0, /device:TPU:1, one launch (start us, length us, event | category | flops | bytes accessed | tf_op | source)
XLA Modules:
  0.0 211.2 jit_solution(10629385373972112505)
XLA Ops:
  8.1 0.9 fusion.45
  9.2 0.7 broadcast_compare_fusion
  9.9 0.7 subtract_clamp_fusion
  10.7 1.2 copy.81
  12.4 0.9 add_bitcast_fusion
  13.3 1.2 fusion.28
  14.6 1.0 fusion.15
  15.6 0.8 convert_add_fusion.1
  16.6 0.8 fusion
  17.4 0.7 fusion.3
  18.1 1.2 fusion.9
  19.3 0.9 copy-done
  20.2 4.7 %convolution_convert_fusion = bf16[512,5120]{1,0:T(8,128)(2,1)} fusion(bf16[512,384]{0,1:T(8,128)(2,1)S(1)} %bitcast.97, bf16[384,5120]{1,0:T(8,128)(2,1)S(1)} %copy-done), kind=kOutput, calls=%fused_computation.3 | convolution fusion | flops 2015887360 | bytes 9568256 | tf_op jit(solution)/shard_map/dot_general | solution.py:117
  25.6 0.5 all-gather.5.cloned.1.call-update
  26.2 0.7 fusion.60
  34.6 0.7 fusion.59
  35.3 0.6 iota_compare_fusion.4
  35.9 0.7 iota_compare_fusion.5
  36.6 0.6 iota_compare_fusion.6
  37.3 0.7 iota_compare_fusion.7
  38.9 0.9 fusion.8
  39.8 1.4 copy.89
  41.2 8.6 %all-to-all-start = ((bf16[16,128,1,256]{3,1,2,0:T(8,128)(2,1)}), bf16[16,128,1,256]{3,1,2,0:T(8,128)(2,1)S(1)}, u32[]{:S(2)}, u32[]{:S(2)}) async-start(bf16[16,128,1,256]{3,1,2,0:T(8,128)(2,1)} %copy.89), calls=%async_computation | async-start | bytes 2097152 | tf_op jit(solution)/shard_map/all_to_all | solution.py:108
  49.9 18.8 %all-to-all-done = bf16[16,128,1,256]{3,1,2,0:T(8,128)(2,1)S(1)} async-done(((bf16[16,128,1,256]{3,1,2,0:T(8,128)(2,1)}), bf16[16,128,1,256]{3,1,2,0:T(8,128)(2,1)S(1)}, u32[]{:S(2)}, u32[]{:S(2)}) %all-to-all-start) | async-done | bytes 1048608 | tf_op jit(solution)/shard_map/all_to_all | solution.py:108
  68.7 0.7 fusion.12
  69.4 0.7 copy.91
  70.1 35.0 %all-reduce.3.cloned.1.call-done = bf16[512,5120]{1,0:T(8,128)(2,1)} async-done(((bf16[512,5120]{1,0:T(8,128)(2,1)}), bf16[512,5120]{1,0:T(8,128)(2,1)}) %all-reduce.3.cloned.1.call-update) | async-done | bytes 5242896 | tf_op jit(solution)/shard_map/psum | solution.py:116
  105.2 5.8 %multiply_reduce_fusion = f32[512]{0:T(512)S(1)} fusion(bf16[512,5120]{1,0:T(8,128)(2,1)} %all-reduce.3.cloned.1.call-done, bf16[512,5120]{1,0:T(8,128)(2,1)} %param.24), kind=kLoop, calls=%fused_computation.1 | loop fusion | flops 13106688 | bytes 10487808 | tf_op jit(solution)/shard_map/reduce_sum | solution.py:30
  111.0 3.9 %all-gather.3.cloned.1.call-done = bf16[5120,864]{1,0:T(8,128)(2,1)} async-done(((bf16[320,864]{1,0:T(8,128)(2,1)}), bf16[5120,864]{1,0:T(8,128)(2,1)}) %all-gather.3.cloned.1.call-update) | async-done | bytes 8847376 | tf_op jit(solution)/shard_map/all_gather | solution.py:56
  114.9 12.1 %fusion.58 = f32[512,864]{0,1:T(8,128)S(1)} fusion(bf16[5120,864]{1,0:T(8,128)(2,1)} %all-gather.3.cloned.1.call-done, bf16[512,5120]{1,0:T(8,128)(2,1)} %all-reduce.3.cloned.1.call-done, bf16[512,5120]{1,0:T(8,128)(2,1)} %param.24, f32[5120]{0:T(1024)S(1)} %copy-done.4, f32[512]{0:T(512)S(1)} %add_rsqrt_fusion), kind=kOutput, calls=%fused_computation.105 | convolution fusion | flops 4545576960 | bytes 21125120 | tf_op jit(solution)/shard_map/dot_general | solution.py:120
  127.0 64.0 %all-gather.5.cloned.1.call-done = bf16[5120,864]{1,0:T(8,128)(2,1)} async-done(((bf16[320,864]{1,0:T(8,128)(2,1)}), bf16[5120,864]{1,0:T(8,128)(2,1)}) %all-gather.5.cloned.1.call-update) | async-done | bytes 8847376 | tf_op jit(solution)/shard_map/all_gather | solution.py:57
  191.0 12.7 %multiply_convert_fusion.1 = bf16[512,864]{0,1:T(8,128)(2,1)} fusion(f32[512,864]{0,1:T(8,128)S(1)} %fusion.58, bf16[5120,864]{1,0:T(8,128)(2,1)} %all-gather.5.cloned.1.call-done, bf16[512,5120]{1,0:T(8,128)(2,1)} %all-reduce.3.cloned.1.call-done, bf16[512,5120]{1,0:T(8,128)(2,1)} %param.24, f32[5120]{0:T(1024)S(1)} %copy-done.4, f32[512]{0:T(512)S(1)} %add_rsqrt_fusion), kind=kOutput, calls=%fused_computation.11 | convolution fusion | flops 4548231168 | bytes 22009856 | tf_op jit(solution)/shard_map/dot_general | solution.py:121
  (35 shorter events, 2.7 us)
Async XLA Ops:
  8.0 97.2 %all-reduce.3.cloned.1.call-start = ((), (), s32[]{:S(2)}) async-start(), calls=%async_computation.1 | async-start | bytes 10485760 | tf_op jit(solution)/shard_map/psum | solution.py:116
  15.6 2.5 %copy-start.1 = (bf16[512,128]{1,0:T(8,128)(2,1)S(1)}, bf16[512,128]{1,0:T(8,128)(2,1)}, u32[]{:S(2)}) copy-start(bf16[512,128]{1,0:T(8,128)(2,1)} %param.16) | copy-start | bytes 393220
  15.6 2.5 %copy-start.3 = (f32[128]{0:T(128)S(1)}, f32[128]{0:T(128)}, u32[]{:S(2)}) copy-start(f32[128]{0:T(128)} %param.19) | copy-start | bytes 1540
  18.1 2.1 %copy-start = (bf16[384,5120]{1,0:T(8,128)(2,1)S(1)}, bf16[384,5120]{1,0:T(8,128)(2,1)}, u32[]{:S(2)}) copy-start(bf16[384,5120]{1,0:T(8,128)(2,1)} %param.23) | copy-start | bytes 11796484
  25.0 24.8 %copy-start.2 = (s32[16,4]{0,1:T(4,128)S(1)}, s32[16,4]{0,1:T(4,128)}, u32[]{:S(2)}) copy-start(s32[16,4]{0,1:T(4,128)} %param.22) | copy-start | bytes 772
  25.0 89.9 %all-gather.3.cloned.1.call-start = ((), (), s32[]{:S(2)}) async-start(), calls=%async_computation.2 | async-start | bytes 9748480 | tf_op jit(solution)/shard_map/all_gather | solution.py:56
  25.6 165.4 %all-gather.5.cloned.1.call-start = ((), (), s32[]{:S(2)}) async-start(), calls=%async_computation.3 | async-start | bytes 9748480 | tf_op jit(solution)/shard_map/all_gather | solution.py:57
  41.2 27.5 %all-to-all-start = ((bf16[16,128,1,256]{3,1,2,0:T(8,128)(2,1)}), bf16[16,128,1,256]{3,1,2,0:T(8,128)(2,1)S(1)}, u32[]{:S(2)}, u32[]{:S(2)}) async-start(bf16[16,128,1,256]{3,1,2,0:T(8,128)(2,1)} %copy.89), calls=%async_computation | async-start | bytes 2097152 | tf_op jit(solution)/shard_map/all_to_all | solution.py:108
  70.1 44.8 %copy-start.4 = (f32[5120]{0:T(1024)S(1)}, f32[5120]{0:T(1024)}, u32[]{:S(2)}) copy-start(f32[5120]{0:T(1024)} %param.25) | copy-start | bytes 61444
Sparse Core Ops, SparseCore 0:
  25.1 80.0 all-reduce.2
Sparse Core Ops, SparseCore 1:
  27.6 87.3 all-gather.2
  116.9 74.0 all-gather.4
where the time goes:
time: 212 us; the launch traced here: 211 us
  waiting for transfers between devices  123 us (58%)
  matrix products  33.1 us (16%)
  between operations  23.5 us (11%)
  other arithmetic  16.9 us (8%)
  starting transfers between devices  8.73 us (4%)
  local copies, waits for them, and re-layouts  6.03 us (3%)
    all_gather x1, waiting for transfers between devices, shards(): wu_full = lax.all_gather(w_up, 'req', axis=0, tiled=True)  64 us
    psum x1, waiting for transfers between devices, shards(): lax.psum(jnp.dot(attended, w_out, preferred_element_type=jnp.float32).ast...  35 us
    all_to_all x1, waiting for transfers between devices, shards(): lax.all_to_all(kv_send, 'req', split_axis=0, concat_axis=0, tiled=True)  18.8 us
    dot_general x1, matrix products, shards(): up_acc = jnp.dot(normed, wu_full, preferred_element_type=jnp.float32)  12.7 us
    dot_general x1, matrix products, shards(): gate_acc = jnp.dot(normed, wg_full, preferred_element_type=jnp.float32)  12.1 us
    all_to_all x1, starting transfers between devices, shards(): lax.all_to_all(kv_send, 'req', split_axis=0, concat_axis=0, tiled=True)  8.61 us
    reduce_sum x1, other arithmetic, normalize(): scale_row = lax.rsqrt(jnp.mean(state * state, axis=-1, keepdims=True) + EPS)  5.83 us
    dot_general x1, matrix products, shards(): jnp.dot(attended, w_out, preferred_element_type=jnp.float32)  4.72 us
  transfers between devices with their start and end apart: 4, of which 4 were waited for; matrix products, arithmetic and copies ran while one was open for 13% of the time, Pallas kernels for 0%

commit v1 on v0

--- a/solution.py
+++ b/solution.py
@@ -54,7 +54,9 @@
     q_heads = q_pre.shape[1] // HD
     group_size = q_heads // kv_heads
     wg_full = lax.all_gather(w_gate, "req", axis=0, tiled=True)
-    wu_full = lax.all_gather(w_up, "req", axis=0, tiled=True)
+    wu_full = jnp.concatenate(
+        lax.all_to_all(jnp.stack([w_up] * lax.axis_size("req")), "req", 0, 0), axis=0
+    )
     own_lens = lax.dynamic_index_in_dim(lengths, me_req, 0, keepdims=False)
     own_pages = lax.dynamic_index_in_dim(page_table, me_req, 0, keepdims=False)
     own_owner = own_pages // REQS

time: 212 us -> 257 us (1.21)
  blocking collectives: 0 us -> 28.5 us
  waiting for transfers between devices: 123 us -> 139 us
  local copies, waits for them, and re-layouts: 6.03 us -> 9.79 us
  starting transfers between devices: 8.73 us -> 5.35 us
    all_gather x1, waiting for transfers between devices: 3.88 us -> 102 us  [shards(): wg_full = lax.all_gather(w_gate, 'req', axis=0, tiled=True)]
    all_gather x1 -> x0, waiting for transfers between devices: 64 us -> none  [shards(): wu_full = lax.all_gather(w_up, 'req', axis=0, tiled=True)]
    all_to_all x0 -> x1, blocking collectives: none -> 28.5 us  [shards(): lax.all_to_all(kv_send, 'req', split_axis=0, concat_axis=0, tiled=True)]
    psum x1, waiting for transfers between devices: 35 us -> 25.8 us  [shards(): lax.psum(jnp.dot(attended, w_out, preferred_element_type=jnp.float32).ast...]
    all_to_all x1, waiting for transfers between devices: 18.8 us -> 11.5 us  [shards(): lax.all_to_all(jnp.stack([w_up] * lax.axis_size('req')), 'req', 0, 0)]
    another operation x0 -> x1, local copies, waits for them, and re-layouts: none -> 4.86 us  [shards(): jnp.stack([w_up] * lax.axis_size('req'))]
    all_to_all x1, starting transfers between devices: 8.61 us -> 5.27 us  [shards(): lax.all_to_all(jnp.stack([w_up] * lax.axis_size('req')), 'req', 0, 0)]
  transfers between devices with their start and end apart: 4 -> 3, of which waited for: 4 -> 3; matrix products, arithmetic and copies ran while one was open for 13% -> 12% of each run, Pallas kernels for 0% -> 0%
where the time goes in v1:
time: 257 us; the launch traced here: 256 us
  waiting for transfers between devices  139 us (54%)
  matrix products  33 us (13%)
  blocking collectives  28.5 us (11%)
  between operations  23.2 us (9%)
  other arithmetic  16.8 us (7%)
  local copies, waits for them, and re-layouts  9.79 us (4%)
  starting transfers between devices  5.35 us (2%)
    all_gather x1, waiting for transfers between devices, shards(): wg_full = lax.all_gather(w_gate, 'req', axis=0, tiled=True)  102 us
    all_to_all x1, blocking collectives, shards(): lax.all_to_all(kv_send, 'req', split_axis=0, concat_axis=0, tiled=True)  28.5 us
    psum x1, waiting for transfers between devices, shards(): lax.psum(jnp.dot(attended, w_out, preferred_element_type=jnp.float32).ast...  25.8 us
    dot_general x1, matrix products, shards(): up_acc = jnp.dot(normed, wu_full, preferred_element_type=jnp.float32)  12.7 us
    dot_general x1, matrix products, shards(): gate_acc = jnp.dot(normed, wg_full, preferred_element_type=jnp.float32)  12.1 us
    all_to_all x1, waiting for transfers between devices, shards(): lax.all_to_all(jnp.stack([w_up] * lax.axis_size('req')), 'req', 0, 0)  11.5 us
    reduce_sum x1, other arithmetic, normalize(): scale_row = lax.rsqrt(jnp.mean(state * state, axis=-1, keepdims=True) + EPS)  5.83 us
    all_to_all x1, starting transfers between devices, shards(): lax.all_to_all(jnp.stack([w_up] * lax.axis_size('req')), 'req', 0, 0)  5.27 us
  transfers between devices with their start and end apart: 3, of which 3 were waited for; matrix products, arithmetic and copies ran while one was open for 12% of the time, Pallas kernels for 0%

profile of v1, /device:TPU:1, one launch (start us, length us, event | category | flops | bytes accessed | tf_op | source)
XLA Modules:
  0.0 255.9 jit_solution(3184877121683113787)
XLA Ops:
  8.1 0.7 broadcast_compare_fusion
  8.8 0.7 subtract_clamp_fusion
  9.4 0.9 fusion.45
  10.7 1.0 fusion.15
  11.7 0.9 add_bitcast_fusion
  12.6 0.5 multiply_cosine_fusion.1
  13.2 1.2 fusion.28
  14.4 1.2 copy.81
  15.6 0.8 convert_add_fusion.1
  16.6 0.8 fusion
  17.4 0.7 fusion.3
  18.1 1.2 fusion.9
  19.3 0.9 copy-done
  20.2 4.6 %convolution_convert_fusion = bf16[512,5120]{1,0:T(8,128)(2,1)} fusion(bf16[512,384]{0,1:T(8,128)(2,1)S(1)} %bitcast.98, bf16[384,5120]{1,0:T(8,128)(2,1)S(1)} %copy-done), kind=kOutput, calls=%fused_computation.3 | convolution fusion | flops 2015887360 | bytes 9568256 | tf_op jit(solution)/shard_map/dot_general | solution.py:119
  25.5 0.6 fusion.60
  33.5 0.6 fusion.59
  34.1 0.6 iota_compare_fusion.7
  34.8 0.7 iota_compare_fusion.4
  35.5 0.6 iota_compare_fusion.5
  36.0 0.6 iota_compare_fusion.6
  37.6 0.9 fusion.8
  38.9 28.5 %all_to_all.10 = bf16[16,128,1,256]{3,1,2,0:T(8,128)(2,1)S(1)} all-to-all(bf16[16,128,1,256]{3,1,2,0:T(8,128)(2,1)S(1)} %copy.89), channel_id=1, replica_groups=mesh['req'=16,'mp'=8] {'req'}, dimensions={0} | all-to-all | bytes 2097152 | tf_op jit(solution)/shard_map/all_to_all | solution.py:110
  67.5 4.9 %stack.12 = bf16[16,320,864]{2,1,0:T(8,128)(2,1)} broadcast(bf16[320,864]{1,0:T(8,128)(2,1)S(1)} %copy-done.1), dimensions={1,2} | broadcast | bytes 9400320 | tf_op jit(solution)/shard_map/stack | solution.py:58
  72.3 5.3 %all-to-all-start = ((bf16[16,320,864]{2,1,0:T(8,128)(2,1)}), bf16[16,320,864]{2,1,0:T(8,128)(2,1)}, u32[]{:S(2)}, u32[]{:S(2)}) async-start(bf16[16,320,864]{2,1,0:T(8,128)(2,1)} %stack.12), calls=%async_computation | async-start | bytes 18350080 | tf_op jit(solution)/shard_map/all_to_all | solution.py:58
  77.7 0.7 fusion.12
  78.4 0.7 copy.91
  79.1 25.8 %all-reduce.3.cloned.1.call-done = bf16[512,5120]{1,0:T(8,128)(2,1)} async-done(((bf16[512,5120]{1,0:T(8,128)(2,1)}), bf16[512,5120]{1,0:T(8,128)(2,1)}) %all-reduce.3.cloned.1.call-update) | async-done | bytes 5242896 | tf_op jit(solution)/shard_map/psum | solution.py:118
  104.9 5.8 %multiply_reduce_fusion = f32[512]{0:T(512)S(1)} fusion(bf16[512,5120]{1,0:T(8,128)(2,1)} %all-reduce.3.cloned.1.call-done, bf16[512,5120]{1,0:T(8,128)(2,1)} %param.24), kind=kLoop, calls=%fused_computation.1 | loop fusion | flops 13106688 | bytes 10487808 | tf_op jit(solution)/shard_map/reduce_sum | solution.py:30
  110.7 101.5 %all-gather.2.cloned.1.call-done = bf16[5120,864]{1,0:T(8,128)(2,1)} async-done(((bf16[320,864]{1,0:T(8,128)(2,1)}), bf16[5120,864]{1,0:T(8,128)(2,1)}) %all-gather.2.cloned.1.call-update) | async-done | bytes 8847376 | tf_op jit(solution)/shard_map/all_gather | solution.py:56
  212.2 12.1 %fusion.58 = f32[512,864]{0,1:T(8,128)S(1)} fusion(bf16[5120,864]{1,0:T(8,128)(2,1)} %all-gather.2.cloned.1.call-done, bf16[512,5120]{1,0:T(8,128)(2,1)} %all-reduce.3.cloned.1.call-done, bf16[512,5120]{1,0:T(8,128)(2,1)} %param.24, f32[5120]{0:T(1024)S(1)} %copy-done.5, f32[512]{0:T(512)S(1)} %add_rsqrt_fusion), kind=kOutput, calls=%fused_computation.105 | convolution fusion | flops 4545576960 | bytes 21125120 | tf_op jit(solution)/shard_map/dot_general | solution.py:122
  224.3 11.5 %all-to-all-done = bf16[16,320,864]{2,1,0:T(8,128)(2,1)} async-done(((bf16[16,320,864]{2,1,0:T(8,128)(2,1)}), bf16[16,320,864]{2,1,0:T(8,128)(2,1)}, u32[]{:S(2)}, u32[]{:S(2)}) %all-to-all-start) | async-done | bytes 8847392 | tf_op jit(solution)/shard_map/all_to_all | solution.py:58
  235.8 12.7 %multiply_convert_fusion.1 = bf16[512,864]{0,1:T(8,128)(2,1)} fusion(f32[512,864]{0,1:T(8,128)S(1)} %fusion.58, bf16[5120,864]{1,0:T(8,128)(2,1)} %bitcast.16, bf16[512,5120]{1,0:T(8,128)(2,1)} %all-reduce.3.cloned.1.call-done, bf16[512,5120]{1,0:T(8,128)(2,1)} %param.24, f32[5120]{0:T(1024)S(1)} %copy-done.5, f32[512]{0:T(512)S(1)} %add_rsqrt_fusion), kind=kOutput, calls=%fused_computation.11 | convolution fusion | flops 4548231168 | bytes 22009856 | tf_op jit(solution)/shard_map/dot_general | solution.py:123
  (36 shorter events, 2.5 us)
Async XLA Ops:
  8.0 96.9 %all-reduce.3.cloned.1.call-start = ((), (), s32[]{:S(2)}) async-start(), calls=%async_computation.2 | async-start | bytes 10485760 | tf_op jit(solution)/shard_map/psum | solution.py:118
  15.6 2.5 copy-start.2
  15.6 2.5 copy-start.4
  18.1 2.1 copy-start
  24.9 42.6 %copy-start.1 = (bf16[320,864]{1,0:T(8,128)(2,1)S(1)}, bf16[320,864]{1,0:T(8,128)(2,1)}, u32[]{:S(2)}) copy-start(bf16[320,864]{1,0:T(8,128)(2,1)} %param.27) | copy-start | bytes 1658884
  24.9 187.4 %all-gather.2.cloned.1.call-start = ((), (), s32[]{:S(2)}) async-start(), calls=%async_computation.3 | async-start | bytes 9748480 | tf_op jit(solution)/shard_map/all_gather | solution.py:56
  72.3 5.3 %copy-start.3 = (s32[16,4]{0,1:T(4,128)S(1)}, s32[16,4]{0,1:T(4,128)}, u32[]{:S(2)}) copy-start(s32[16,4]{0,1:T(4,128)} %param.22) | copy-start | bytes 772
  72.3 163.5 %all-to-all-start = ((bf16[16,320,864]{2,1,0:T(8,128)(2,1)}), bf16[16,320,864]{2,1,0:T(8,128)(2,1)}, u32[]{:S(2)}, u32[]{:S(2)}) async-start(bf16[16,320,864]{2,1,0:T(8,128)(2,1)} %stack.12), calls=%async_computation | async-start | bytes 18350080 | tf_op jit(solution)/shard_map/all_to_all | solution.py:58
  79.1 133.1 %copy-start.5 = (f32[5120]{0:T(1024)S(1)}, f32[5120]{0:T(1024)}, u32[]{:S(2)}) copy-start(f32[5120]{0:T(1024)} %param.25) | copy-start | bytes 61444
Sparse Core Ops, SparseCore 0:
  25.0 79.8 all-reduce.2
Sparse Core Ops, SparseCore 1:
  27.5 184.7 all-gather.1
